TPU v7x, 32 devices: a whole 2x2x4 slice. The times are simulated.
32 devices in a mesh: dp: 8 (over y, x, core), fsdp: 4 (over z).
Axes of the slice: x: 2, y: 2, z: 4, core: 2. Of those that a mesh axis runs over, the one named last changes fastest.
Arguments:
- gene_ids: int32 [32, 2048], P(('dp', 'fsdp')), may hold values from 0 to 12799
- expr_bins: int32 [32, 2048], P(('dp', 'fsdp')), may hold values from 0 to 63
- study_ids: int32 [32], P(('dp', 'fsdp')), may hold values from 0 to 63
- lengths: int32 [32], P(('dp', 'fsdp')), may hold values from 256 to 2048, as said below
- prior_embed: bfloat16 [32, 2048, 256], P(('dp', 'fsdp')), may hold values from -3 to 3
- cotangent: bfloat16 [32, 2048, 256], P(('dp', 'fsdp')), may hold values from -6 to 6
- gene_table: bfloat16 [12800, 256], P('fsdp'), may hold values from -3 to 3
- expr_table: bfloat16 [64, 256], P('fsdp'), may hold values from -3 to 3
- study_table: bfloat16 [64, 256], P('fsdp'), may hold values from -3 to 3
- position_table: bfloat16 [2048, 256], P('fsdp'), may hold values from -3 to 3
- norm1_gain: bfloat16 [256], P('fsdp'), may hold values from 0.099609375 to 1.8984375
- norm1_shift: bfloat16 [256], P('fsdp'), may hold values from -1.5 to 1.5
- w_qkv: bfloat16 [256, 768], P('fsdp'), may hold values from -0.375 to 0.375
- bias_query: bfloat16 [256], P('fsdp'), may hold values from -1.5 to 1.5
- bias_value: bfloat16 [256], P('fsdp'), may hold values from -1.5 to 1.5
- w_output: bfloat16 [256, 256], P('fsdp'), may hold values from -6 to 6
- bias_output: bfloat16 [256], P('fsdp'), may hold values from -1.5 to 1.5
- norm2_gain: bfloat16 [256], P('fsdp'), may hold values from 0.099609375 to 1.8984375
- norm2_shift: bfloat16 [256], P('fsdp'), may hold values from -1.5 to 1.5
- w_up_proj: bfloat16 [256, 512], P('fsdp'), may hold values from -0.375 to 0.375
- bias_up: bfloat16 [512], P('fsdp'), may hold values from -1.5 to 1.5
- w_down_proj: bfloat16 [512, 256], P('fsdp'), may hold values from -0.25 to 0.25
- bias_down: bfloat16 [256], P('fsdp'), may hold values from -1.5 to 1.5
Outputs:
- hidden_out: bfloat16 [32, 2048, 256], P(('dp', 'fsdp'))
- grad_gene_table: float32 [12800, 256], P('fsdp')
- update_count: int32 [12800], P('fsdp')
- grad_expr_table: float32 [64, 256], P('fsdp')
- grad_study_table: float32 [64, 256], P('fsdp')
- grad_position_table: float32 [2048, 256], P('fsdp')
- grad_norm1_gain: float32 [256], P('fsdp')
- grad_norm1_shift: float32 [256], P('fsdp')
- grad_w_qkv: float32 [256, 768], P('fsdp')
- grad_bias_query: float32 [256], P('fsdp')
- grad_bias_value: float32 [256], P('fsdp')
- grad_w_output: float32 [256, 256], P('fsdp')
- grad_bias_output: float32 [256], P('fsdp')
- grad_norm2_gain: float32 [256], P('fsdp')
- grad_norm2_shift: float32 [256], P('fsdp')
- grad_w_up_proj: float32 [256, 512], P('fsdp')
- grad_bias_up: float32 [512], P('fsdp')
- grad_w_down_proj: float32 [512, 256], P('fsdp')
- grad_bias_down: float32 [256], P('fsdp')
Inputs may be any that keep to these rules, and one draw needn't show every extreme that they name: Slots from lengths[c] on are padding; some cell has 2048 genes and some 2048 // 8.
All inputs are finite; a program needn't handle non-finite values.
Results may differ from a plain program's by a relative error of at most 0.0082.
Values may be sent and summed in bfloat16 or wider, within the bound.
No kernel may reach another device: no remote copies, remote signals or barrier semaphores. Data moves between devices by JAX's collectives and lax.ppermute only.
A program may use at most 128 MiB of HBM per device.

v0:
```python
import jax
import jax.numpy as jnp
from jax import lax
from jax.sharding import PartitionSpec as P

HEADS = 4
epsilon = 1e-05
highest = lax.Precision.HIGHEST


def normalize(values):
    average = jnp.mean(values, axis=-1, keepdims=True)
    centered = values - average
    variance = jnp.mean(centered * centered, axis=-1, keepdims=True)
    return centered * lax.rsqrt(variance + epsilon)


def norm_back(values, gain, grad):
    unused, pullback = jax.vjp(lambda entries, scale: normalize(entries) * scale, values, gain)
    grad_rows, grad_gain = pullback(grad)
    return (grad_rows, grad_gain, jnp.sum(grad, axis=0))


def matmul(left, right):
    return jnp.dot(left, right, preferred_element_type=jnp.float32)


def weight_grad(left, right):
    return lax.dot_general(
        left, right, (((0,), (0,)), ((), ())), preferred_element_type=jnp.float32
    )


def back_matmul(left, right):
    return lax.dot_general(
        left, right, (((1,), (1,)), ((), ())), preferred_element_type=jnp.float32
    )


def table_grad(hits, grads):
    return lax.dot_general(
        hits, grads, (((0,), (0,)), ((), ())), precision=highest, preferred_element_type=jnp.float32
    )


def attend(query, keys, values, key_mask, block):
    length, heads, head_size = query.shape
    scale = head_size ** (-0.5)
    query_blocks = query.reshape(length // block, block, heads, head_size)

    def one_block(query_block):
        scores = (
            jnp.einsum("qhk,shk->hqs", query_block, keys, preferred_element_type=jnp.float32)
            * scale
        )
        scores = jnp.where(key_mask[None, None, :] > 0, scores, -1000000000.0)
        peak = jnp.max(scores, axis=-1, keepdims=True)
        raised = jnp.exp(scores - peak)
        total = jnp.sum(raised, axis=-1, keepdims=True)
        probs = (raised / total).astype(jnp.bfloat16)
        attended = jnp.einsum("hqs,shk->qhk", probs, values, preferred_element_type=jnp.float32)
        return (attended.astype(jnp.bfloat16), (peak + jnp.log(total))[..., 0])

    attended, log_total = lax.map(one_block, query_blocks)
    return (attended.reshape(length, heads, head_size), log_total)


def attend_back(query, keys, values, key_mask, log_total, grad_attended, block):
    length, heads, head_size = query.shape
    scale = head_size ** (-0.5)
    query_blocks = query.reshape(length // block, block, heads, head_size)
    grad_blocks = grad_attended.reshape(length // block, block, heads, head_size)

    def one_block(carry, embedding_parts):
        grad_keys, grad_values = carry
        query_block, grad_block, log_block = embedding_parts
        scores = (
            jnp.einsum("qhk,shk->hqs", query_block, keys, preferred_element_type=jnp.float32)
            * scale
        )
        scores = jnp.where(key_mask[None, None, :] > 0, scores, -1000000000.0)
        probs = jnp.exp(scores - log_block[..., None])
        probs_low = probs.astype(jnp.bfloat16)
        grad_probs = jnp.einsum(
            "qhk,shk->hqs", grad_block, values, preferred_element_type=jnp.float32
        )
        inner = jnp.sum(probs * grad_probs, axis=-1, keepdims=True)
        grad_scores = (probs * (grad_probs - inner)).astype(jnp.bfloat16)
        grad_query = (
            jnp.einsum("hqs,shk->qhk", grad_scores, keys, preferred_element_type=jnp.float32)
            * scale
        )
        grad_keys = (
            grad_keys
            + jnp.einsum(
                "hqs,qhk->shk", grad_scores, query_block, preferred_element_type=jnp.float32
            )
            * scale
        )
        grad_values = grad_values + jnp.einsum(
            "hqs,qhk->shk", probs_low, grad_block, preferred_element_type=jnp.float32
        )
        return ((grad_keys, grad_values), grad_query)

    starting = jnp.zeros((length, heads, head_size), jnp.float32)
    (grad_keys, grad_values), grad_query = lax.scan(
        one_block, (starting, starting), (query_blocks, grad_blocks, log_total)
    )
    return (grad_query.reshape(length, heads, head_size), grad_keys, grad_values)


def body(
    gene_ids,
    expr_bins,
    study_ids,
    lengths,
    prior_embed,
    cotangent,
    gene_table,
    expr_table,
    study_table,
    position_table,
    norm1_gain,
    norm1_shift,
    w_qkv,
    bias_query,
    bias_value,
    w_output,
    bias_output,
    norm2_gain,
    norm2_shift,
    w_up_proj,
    bias_up,
    w_down_proj,
    bias_down,
):
    (
        full_gene,
        full_expr,
        full_study,
        full_position,
        gain_one,
        shift_one,
        full_qkv,
        query_bias,
        value_bias,
        full_output,
        output_bias,
        gain_two,
        shift_two,
        full_up,
        up_bias,
        full_down,
        down_bias,
    ) = (
        lax.all_gather(gene_table, "fsdp", axis=0, tiled=True),
        lax.all_gather(expr_table, "fsdp", axis=0, tiled=True),
        lax.all_gather(study_table, "fsdp", axis=0, tiled=True),
        lax.all_gather(position_table, "fsdp", axis=0, tiled=True),
        lax.all_gather(norm1_gain, "fsdp", axis=0, tiled=True),
        lax.all_gather(norm1_shift, "fsdp", axis=0, tiled=True),
        lax.all_gather(w_qkv, "fsdp", axis=0, tiled=True),
        lax.all_gather(bias_query, "fsdp", axis=0, tiled=True),
        lax.all_gather(bias_value, "fsdp", axis=0, tiled=True),
        lax.all_gather(w_output, "fsdp", axis=0, tiled=True),
        lax.all_gather(bias_output, "fsdp", axis=0, tiled=True),
        lax.all_gather(norm2_gain, "fsdp", axis=0, tiled=True),
        lax.all_gather(norm2_shift, "fsdp", axis=0, tiled=True),
        lax.all_gather(w_up_proj, "fsdp", axis=0, tiled=True),
        lax.all_gather(bias_up, "fsdp", axis=0, tiled=True),
        lax.all_gather(w_down_proj, "fsdp", axis=0, tiled=True),
        lax.all_gather(bias_down, "fsdp", axis=0, tiled=True),
    )
    cells, length = gene_ids.shape
    width = full_gene.shape[1]
    rows = cells * length
    heads = HEADS
    head_size = width // heads
    block = min(512, length)

    def shaped(array):
        return array.reshape(cells, length, heads, head_size)

    key_mask = (lax.broadcasted_iota(jnp.int32, (cells, length), 1) < lengths[:, None]).astype(
        jnp.float32
    )
    flat_mask = key_mask.reshape(rows, 1)
    embedded = (
        full_gene[gene_ids].astype(jnp.float32)
        + full_expr[expr_bins].astype(jnp.float32)
        + full_study[study_ids].astype(jnp.float32)[:, None, :]
        + full_position.astype(jnp.float32)[None]
        + prior_embed.astype(jnp.float32)
    )
    inputs = (embedded * key_mask[..., None]).reshape(rows, width)
    normed_one = (
        normalize(inputs) * gain_one.astype(jnp.float32) + shift_one.astype(jnp.float32)
    ).astype(jnp.bfloat16)
    mixed = matmul(normed_one, full_qkv)
    query = (mixed[:, :width] + query_bias.astype(jnp.float32)).astype(jnp.bfloat16)
    keys = mixed[:, width : 2 * width].astype(jnp.bfloat16)
    values = (mixed[:, 2 * width :] + value_bias.astype(jnp.float32)).astype(jnp.bfloat16)
    attended, log_total = lax.map(
        lambda embedding_parts: attend(
            embedding_parts[0], embedding_parts[1], embedding_parts[2], embedding_parts[3], block
        ),
        (shaped(query), shaped(keys), shaped(values), key_mask),
    )
    attended = attended.reshape(rows, width)
    branch = matmul(attended, full_output) + output_bias.astype(jnp.float32)
    middle = inputs + branch
    normed_two = (
        normalize(middle) * gain_two.astype(jnp.float32) + shift_two.astype(jnp.float32)
    ).astype(jnp.bfloat16)
    upward = matmul(normed_two, full_up) + up_bias.astype(jnp.float32)
    activated = jax.nn.gelu(upward, approximate=False).astype(jnp.bfloat16)
    result = (middle + (matmul(activated, full_down) + down_bias.astype(jnp.float32))) * flat_mask
    hidden_out = result.astype(jnp.bfloat16).reshape(cells, length, width)
    back_gain_one, back_qkv, back_output, back_gain_two, back_up, back_down = (
        lax.all_gather(norm1_gain, "fsdp", axis=0, tiled=True),
        lax.all_gather(w_qkv, "fsdp", axis=0, tiled=True),
        lax.all_gather(w_output, "fsdp", axis=0, tiled=True),
        lax.all_gather(norm2_gain, "fsdp", axis=0, tiled=True),
        lax.all_gather(w_up_proj, "fsdp", axis=0, tiled=True),
        lax.all_gather(w_down_proj, "fsdp", axis=0, tiled=True),
    )
    grad_result = cotangent.astype(jnp.float32).reshape(rows, width) * flat_mask
    grad_low = grad_result.astype(jnp.bfloat16)
    grad_down_w = weight_grad(activated, grad_low)
    grad_down_b = jnp.sum(grad_result, axis=0)
    grad_activated = back_matmul(grad_low, back_down)
    unused, gelu_pull = jax.vjp(lambda entries: jax.nn.gelu(entries, approximate=False), upward)
    grad_upward = gelu_pull(grad_activated)[0].astype(jnp.bfloat16)
    grad_up_w = weight_grad(normed_two, grad_upward)
    grad_up_b = jnp.sum(grad_upward.astype(jnp.float32), axis=0)
    grad_normed_two = back_matmul(grad_upward, back_up)
    grad_mid_norm, grad_gain_two, grad_shift_two = norm_back(
        middle, back_gain_two.astype(jnp.float32), grad_normed_two
    )
    grad_middle = grad_result + grad_mid_norm
    grad_branch = grad_middle.astype(jnp.bfloat16)
    grad_output_w = weight_grad(attended, grad_branch)
    grad_output_b = jnp.sum(grad_branch.astype(jnp.float32), axis=0)
    grad_attended = back_matmul(grad_branch, back_output).astype(jnp.bfloat16)
    grad_query, grad_keys, grad_values = lax.map(
        lambda embedding_parts: attend_back(
            embedding_parts[0],
            embedding_parts[1],
            embedding_parts[2],
            embedding_parts[3],
            embedding_parts[4],
            embedding_parts[5],
            block,
        ),
        (shaped(query), shaped(keys), shaped(values), key_mask, log_total, shaped(grad_attended)),
    )
    grad_query = grad_query.reshape(rows, width).astype(jnp.bfloat16)
    grad_keys = grad_keys.reshape(rows, width).astype(jnp.bfloat16)
    grad_values = grad_values.reshape(rows, width).astype(jnp.bfloat16)
    grad_mixed = jnp.concatenate([grad_query, grad_keys, grad_values], axis=1)
    grad_qkv_w = weight_grad(normed_one, grad_mixed)
    grad_query_b = jnp.sum(grad_query.astype(jnp.float32), axis=0)
    grad_value_b = jnp.sum(grad_values.astype(jnp.float32), axis=0)
    grad_normed_one = back_matmul(grad_mixed, back_qkv)
    grad_in_norm, grad_gain_one, grad_shift_one = norm_back(
        inputs, back_gain_one.astype(jnp.float32), grad_normed_one
    )
    grad_inputs = (grad_middle + grad_in_norm) * flat_mask
    grad_cells = grad_inputs.reshape(cells, length, width)
    bin_hits = (
        expr_bins.reshape(rows, 1) == lax.broadcasted_iota(jnp.int32, (1, full_expr.shape[0]), 1)
    ).astype(jnp.float32)
    grad_expr = table_grad(bin_hits, grad_inputs)
    study_hits = (
        study_ids[:, None] == lax.broadcasted_iota(jnp.int32, (1, full_study.shape[0]), 1)
    ).astype(jnp.float32)
    grad_study = table_grad(study_hits, jnp.sum(grad_cells, axis=1))
    grad_position = jnp.sum(grad_cells, axis=0)
    flat_ids = gene_ids.reshape(rows)
    vocab = full_gene.shape[0]
    dense_grad = jnp.zeros((vocab, width), jnp.float32).at[flat_ids].add(grad_inputs)
    dense_count = jnp.zeros((vocab,), jnp.float32).at[flat_ids].add(flat_mask[:, 0])
    (
        table_share,
        count_share,
        expr_share,
        study_share,
        position_share,
        gain_one_share,
        shift_one_share,
        qkv_share,
        query_b_share,
        value_b_share,
        output_share,
        output_b_share,
        gain_two_share,
        shift_two_share,
        up_share,
        up_b_share,
        down_share,
        down_b_share,
    ) = (
        lax.psum_scatter(dense_grad, "fsdp", scatter_dimension=0, tiled=True),
        lax.psum_scatter(dense_count, "fsdp", scatter_dimension=0, tiled=True),
        lax.psum_scatter(grad_expr, "fsdp", scatter_dimension=0, tiled=True),
        lax.psum_scatter(grad_study, "fsdp", scatter_dimension=0, tiled=True),
        lax.psum_scatter(grad_position, "fsdp", scatter_dimension=0, tiled=True),
        lax.psum_scatter(grad_gain_one, "fsdp", scatter_dimension=0, tiled=True),
        lax.psum_scatter(grad_shift_one, "fsdp", scatter_dimension=0, tiled=True),
        lax.psum_scatter(grad_qkv_w, "fsdp", scatter_dimension=0, tiled=True),
        lax.psum_scatter(grad_query_b, "fsdp", scatter_dimension=0, tiled=True),
        lax.psum_scatter(grad_value_b, "fsdp", scatter_dimension=0, tiled=True),
        lax.psum_scatter(grad_output_w, "fsdp", scatter_dimension=0, tiled=True),
        lax.psum_scatter(grad_output_b, "fsdp", scatter_dimension=0, tiled=True),
        lax.psum_scatter(grad_gain_two, "fsdp", scatter_dimension=0, tiled=True),
        lax.psum_scatter(grad_shift_two, "fsdp", scatter_dimension=0, tiled=True),
        lax.psum_scatter(grad_up_w, "fsdp", scatter_dimension=0, tiled=True),
        lax.psum_scatter(grad_up_b, "fsdp", scatter_dimension=0, tiled=True),
        lax.psum_scatter(grad_down_w, "fsdp", scatter_dimension=0, tiled=True),
        lax.psum_scatter(grad_down_b, "fsdp", scatter_dimension=0, tiled=True),
    )
    (
        table_sum,
        count_sum,
        expr_sum,
        study_sum,
        position_sum,
        gain_one_sum,
        shift_one_sum,
        qkv_sum,
        query_b_sum,
        value_b_sum,
        output_sum,
        output_b_sum,
        gain_two_sum,
        shift_two_sum,
        up_sum,
        up_b_sum,
        down_sum,
        down_b_sum,
    ) = lax.psum(
        (
            table_share,
            count_share,
            expr_share,
            study_share,
            position_share,
            gain_one_share,
            shift_one_share,
            qkv_share,
            query_b_share,
            value_b_share,
            output_share,
            output_b_share,
            gain_two_share,
            shift_two_share,
            up_share,
            up_b_share,
            down_share,
            down_b_share,
        ),
        "dp",
    )
    return (
        hidden_out,
        table_sum,
        count_sum.astype(jnp.int32),
        expr_sum,
        study_sum,
        position_sum,
        gain_one_sum,
        shift_one_sum,
        qkv_sum,
        query_b_sum,
        value_b_sum,
        output_sum,
        output_b_sum,
        gain_two_sum,
        shift_two_sum,
        up_sum,
        up_b_sum,
        down_sum,
        down_b_sum,
    )


def solution(mesh):
    return jax.shard_map(
        body,
        mesh=mesh,
        in_specs=(
            P(("dp", "fsdp"), None),
            P(("dp", "fsdp"), None),
            P(("dp", "fsdp")),
            P(("dp", "fsdp")),
            P(("dp", "fsdp"), None, None),
            P(("dp", "fsdp"), None, None),
            P("fsdp", None),
            P("fsdp", None),
            P("fsdp", None),
            P("fsdp", None),
            P("fsdp"),
            P("fsdp"),
            P("fsdp", None),
            P("fsdp"),
            P("fsdp"),
            P("fsdp", None),
            P("fsdp"),
            P("fsdp"),
            P("fsdp"),
            P("fsdp", None),
            P("fsdp"),
            P("fsdp", None),
            P("fsdp"),
        ),
        out_specs=(
            P(("dp", "fsdp"), None, None),
            P("fsdp", None),
            P("fsdp"),
            P("fsdp", None),
            P("fsdp", None),
            P("fsdp", None),
            P("fsdp"),
            P("fsdp"),
            P("fsdp", None),
            P("fsdp"),
            P("fsdp"),
            P("fsdp", None),
            P("fsdp"),
            P("fsdp"),
            P("fsdp"),
            P("fsdp", None),
            P("fsdp"),
            P("fsdp", None),
            P("fsdp"),
        ),
        check_vma=False,
    )
```

profile of v0, /device:TPU:0, one launch (start us, length us, event | category | flops | bytes accessed | tf_op | source)
XLA Modules:
  0.0 905.6 jit_solution(10123542352486221909)
XLA Ops:
  20.7 16.2 %all-reduce.21 = (bf16[256]{0:T(256)(128)(2,1)S(1)}, bf16[256]{0:T(256)(128)(2,1)S(1)}, bf16[256]{0:T(256)(128)(2,1)S(1)}, bf16[256]{0:T(256)(128)(2,1)S(1)}, bf...) all-reduce(bf16[256]{0:T(256)(128)(2,1)S(1)} %dynamic-update-slice., ...), channel_id=1, replica_groups=mesh['dp'=8,'fsdp'=4] {'fsdp'}, use_global_device_ids=true, to_apply=%add.1 | all-reduce | flops 2048 | bytes 8192
  49.2 16.0 %all_gather.58 = bf16[64,256]{1,0:T(8,128)(2,1)S(1)} all-gather(bf16[16,256]{1,0:T(8,128)(2,1)} %param.34), channel_id=1, replica_groups=mesh['dp'=8,'fsdp'=4] {'fsdp'}, dimensions={0}, use_global_device_ids=true | all-gather | bytes 40960 | tf_op jit(solution)/shard_map/all_gather | solution.py:157
  76.3 15.8 %all_gather.59 = bf16[64,256]{1,0:T(8,128)(2,1)S(1)} all-gather(bf16[16,256]{1,0:T(8,128)(2,1)S(1)} %copy-done.55), channel_id=1, replica_groups=mesh['dp'=8,'fsdp'=4] {'fsdp'}, dimensions={0}, use_global_device_ids=true | all-gather | bytes 40960 | tf_op jit(solution)/shard_map/all_gather | solution.py:158
  92.2 18.9 %all_gather.66 = bf16[256,256]{1,0:T(8,128)(2,1)} all-gather(bf16[64,256]{1,0:T(8,128)(2,1)S(1)} %copy-done.49), channel_id=1, replica_groups=mesh['dp'=8,'fsdp'=4] {'fsdp'}, dimensions={0}, use_global_device_ids=true | all-gather | bytes 163840 | tf_op jit(solution)/shard_map/all_gather | solution.py:165
  111.1 22.1 %all_gather.70 = bf16[256,512]{1,0:T(8,128)(2,1)} all-gather(bf16[64,512]{1,0:T(8,128)(2,1)S(1)} %copy-done.44), channel_id=1, replica_groups=mesh['dp'=8,'fsdp'=4] {'fsdp'}, dimensions={0}, use_global_device_ids=true | all-gather | bytes 327680 | tf_op jit(solution)/shard_map/all_gather | solution.py:169
  133.2 16.9 %all_gather.72 = bf16[512,256]{1,0:T(8,128)(2,1)} all-gather(bf16[128,256]{1,0:T(8,128)(2,1)S(1)} %copy-done.45), channel_id=1, replica_groups=mesh['dp'=8,'fsdp'=4] {'fsdp'}, dimensions={0}, use_global_device_ids=true | all-gather | bytes 327680 | tf_op jit(solution)/shard_map/all_gather | solution.py:171
  150.7 17.1 %all_gather.63 = bf16[256,768]{1,0:T(8,128)(2,1)S(1)} all-gather(bf16[64,768]{1,0:T(8,128)(2,1)} %param.39), channel_id=1, replica_groups=mesh['dp'=8,'fsdp'=4] {'fsdp'}, dimensions={0}, use_global_device_ids=true | all-gather | bytes 491520 | tf_op jit(solution)/shard_map/all_gather | solution.py:162
  167.8 12.3 %gather_fusion = bf16[2048,256]{1,0:T(8,128)(2,1)} fusion(bf16[12800,256]{1,0:T(8,128)(2,1)} %all-gather.4.cloned.1.call-done, s32[2048]{0:T(1024)S(1)} %broadcast_clamp_fusion.1), kind=kCustom, calls=%fused_computation | custom fusion | bytes 2105344 | tf_op jit(solution)/shard_map/gather | solution.py:189
  191.9 53.9 %while.49 = (s32[]{:T(128)}, bf16[4,512,4,64]{1,3,2,0:T(8,128)(2,1)}, f32[4,4,512]{2,1,0:T(4,128)S(1)}, bf16[4,512,4,64]{1,3,2,0:T(8,128)(2,1)}, bf16[2048,4,64]...) while((s32[]{:T(128)}, bf16[4,512,4,64]{1,3,2,0:T(8,128)(2,1)}, ...), condition=%wide.region_5.6_spmd.clone, body=%wide.region_2.5_spmd.clone.sunk | while | flops 1124208640 | bytes 53026924 | solution.py:64
  249.5 10.9 %multiply_convert_fusion.1 = (bf16[2048,512]{1,0:T(8,128)(2,1)}, f32[2048,512]{1,0:T(8,128)S(1)}, f32[2048,512]{1,0:T(8,128)S(1)}) fusion(f32[512]{0:T(512)S(1)} %bitcast.190, bf16[256,512]{1,0:T(8,128)(2,1)S(1)} %copy-done.26, f32[2048,256]{0,1:T(8,128)S(1)} %get-tuple-element.435, f32[256]{0:T(256)S(1)} %copy-done.72, f32[256]{0:T(256)S(1)} %copy-done.64, ...), kind=kOutput, calls=%fused_computation.63 | convolution fusion | flops 608698368 | bytes 12865536 | tf_op jit(solution)/shard_map/dot_general | solution.py:25
  297.0 166.8 %while.50 = (s32[]{:T(128)}, f32[2048,4,64]{0,2,1:T(8,128)}, f32[2048,4,64]{0,2,1:T(8,128)}, bf16[4,512,4,64]{1,3,2,0:T(8,128)(2,1)}, bf16[4,512,4,64]{1,3,2,0:T...) while((s32[]{:T(128)}, f32[2048,4,64]{0,2,1:T(8,128)}, ...), condition=%wide.region_12.13_spmd.clone, body=%wide.region_10.12_spmd.clone.sunk | while | flops 2750025728 | bytes 172556464 | solution.py:106
  306.8 9.5 %multiply_reduce_fusion.8 = (f32[4,512]{1,0:T(4,128)S(1)}, f32[4,512,2048]{2,1,0:T(8,128)}) fusion(f32[4,512,2048]{2,1,0:T(8,128)S(1)} %fusion.154, f32[4,512]{1,0:T(4,128)S(1)} %dynamic-slice_bitcast_fusion.2, pred[2048]{0:T(1024)(128)(4,1)S(1)} %convert_compare_fusion.5, bf16[2048,4,64]{0,2,1:T(8,128)(2,1)S(1)} %get-tuple-element.611, ...), kind=kOutput, calls=%fused_computation.25.clone.1 | convolution fusion | flops 557840384 | bytes 34883588 | tf_op jit(solution)/shard_map/while/body/eval_jaxpr/while/body/eval_jaxpr/qhk,shk->hqs/dot_general | solution.py:84
  316.4 10.8 %multiply_convert_fusion.3 = bf16[4,512,2048]{2,1,0:T(8,128)(2,1)} fusion(f32[4,512,2048]{2,1,0:T(8,128)} %get-tuple-element.553, f32[4,512,2048]{2,1,0:T(8,128)S(1)} %fusion.154, f32[4,512]{1,0:T(4,128)S(1)} %get-tuple-element.554, f32[4,512]{1,0:T(4,128)S(1)} %dynamic-slice_bitcast_fusion.2, pred[2048]{0:T(1024)(128)(4,1)S(1)} %convert_compare_fusion.5), kind=kLoop, calls=%fused_computation.24.clone.1 | loop fusion | flops 25165824 | bytes 41961472 | tf_op jit(solution)/shard_map/while/body/eval_jaxpr/while/body/eval_jaxpr/convert_element_type | solution.py:88
  357.7 10.7 %multiply_convert_fusion.3 = bf16[4,512,2048]{2,1,0:T(8,128)(2,1)} fusion(f32[4,512,2048]{2,1,0:T(8,128)} %get-tuple-element.553, f32[4,512,2048]{2,1,0:T(8,128)S(1)} %fusion.154, f32[4,512]{1,0:T(4,128)S(1)} %get-tuple-element.554, f32[4,512]{1,0:T(4,128)S(1)} %dynamic-slice_bitcast_fusion.2, pred[2048]{0:T(1024)(128)(4,1)S(1)} %convert_compare_fusion.5), kind=kLoop, calls=%fused_computation.24.clone.1 | loop fusion | flops 25165824 | bytes 41961472 | tf_op jit(solution)/shard_map/while/body/eval_jaxpr/while/body/eval_jaxpr/convert_element_type | solution.py:88
  390.0 9.5 %multiply_reduce_fusion.8 = (f32[4,512]{1,0:T(4,128)S(1)}, f32[4,512,2048]{2,1,0:T(8,128)}) fusion(f32[4,512,2048]{2,1,0:T(8,128)S(1)} %fusion.154, f32[4,512]{1,0:T(4,128)S(1)} %dynamic-slice_bitcast_fusion.2, pred[2048]{0:T(1024)(128)(4,1)S(1)} %convert_compare_fusion.5, bf16[2048,4,64]{0,2,1:T(8,128)(2,1)S(1)} %get-tuple-element.611, ...), kind=kOutput, calls=%fused_computation.25.clone.1 | convolution fusion | flops 557840384 | bytes 34883588 | tf_op jit(solution)/shard_map/while/body/eval_jaxpr/while/body/eval_jaxpr/qhk,shk->hqs/dot_general | solution.py:84
  399.5 10.7 %multiply_convert_fusion.3 = bf16[4,512,2048]{2,1,0:T(8,128)(2,1)} fusion(f32[4,512,2048]{2,1,0:T(8,128)} %get-tuple-element.553, f32[4,512,2048]{2,1,0:T(8,128)S(1)} %fusion.154, f32[4,512]{1,0:T(4,128)S(1)} %get-tuple-element.554, f32[4,512]{1,0:T(4,128)S(1)} %dynamic-slice_bitcast_fusion.2, pred[2048]{0:T(1024)(128)(4,1)S(1)} %convert_compare_fusion.5), kind=kLoop, calls=%fused_computation.24.clone.1 | loop fusion | flops 25165824 | bytes 41961472 | tf_op jit(solution)/shard_map/while/body/eval_jaxpr/while/body/eval_jaxpr/convert_element_type | solution.py:88
  441.4 10.7 %multiply_convert_fusion.3 = bf16[4,512,2048]{2,1,0:T(8,128)(2,1)} fusion(f32[4,512,2048]{2,1,0:T(8,128)} %get-tuple-element.553, f32[4,512,2048]{2,1,0:T(8,128)S(1)} %fusion.154, f32[4,512]{1,0:T(4,128)S(1)} %get-tuple-element.554, f32[4,512]{1,0:T(4,128)S(1)} %dynamic-slice_bitcast_fusion.2, pred[2048]{0:T(1024)(128)(4,1)S(1)} %convert_compare_fusion.5), kind=kLoop, calls=%fused_computation.24.clone.1 | loop fusion | flops 25165824 | bytes 41961472 | tf_op jit(solution)/shard_map/while/body/eval_jaxpr/while/body/eval_jaxpr/convert_element_type | solution.py:88
  490.6 17.5 %scatter_custom_fusion = f32[12800,256]{1,0:T(8,128)} fusion(s32[2048]{0:T(1024)S(1)} %bitcast.187, f32[2048,256]{1,0:T(8,128)} %copy.90, f32[]{:T(128)} %constant.51.clone.1), kind=kCustom, calls=%fused_computation.57 | custom fusion | flops 524288 | bytes 13107712 | tf_op jit(solution)/shard_map/scatter-add | solution.py:281
  513.3 26.0 %reduce-scatter.15.cloned.1.call-done = f32[512,256]{0,1:T(8,128)} async-done(((f32[2048,256]{0,1:T(8,128)}), f32[512,256]{0,1:T(8,128)}) %reduce-scatter.15.cloned.1.call-update) | async-done | bytes 524304 | tf_op jit(solution)/shard_map/reduce_scatter | solution.py:307
  539.2 222.0 %reduce-scatter.9.cloned.1.call-done = f32[3200,256]{1,0:T(8,128)} async-done(((f32[12800,256]{1,0:T(8,128)}), f32[3200,256]{1,0:T(8,128)}) %reduce-scatter.9.cloned.1.call-update) | async-done | bytes 3276816 | tf_op jit(solution)/shard_map/reduce_scatter | solution.py:303
  761.3 11.3 %scatter_custom_fusion.1 = f32[12800]{0:T(1024)S(1)} fusion(s32[2048]{0:T(1024)S(1)} %bitcast.188, f32[2048]{0:T(1024)S(1)} %copy-done.36, f32[]{:T(128)} %constant.51.clone.1), kind=kCustom, calls=%fused_computation.126 | custom fusion | flops 2048 | bytes 51204 | tf_op jit(solution)/shard_map/scatter-add | solution.py:282
  780.6 19.4 %all-reduce.20 = (f32[12800]{0:T(1024)S(1)}, f32[256]{0:T(256)S(1)}, f32[256]{0:T(256)S(1)}, f32[256]{0:T(256)S(1)}, f32[256]{0:T(256)S(1)}, /*index=5*/f32[256]...) all-reduce(f32[12800]{0:T(1024)S(1)} %scatter_custom_fusion.1, ...), channel_id=3, replica_groups=mesh['dp'=8,'fsdp'=4] {'fsdp'}, use_global_device_ids=true, to_apply=%region_19.20.clone | all-reduce | flops 15360 | bytes 122880
  804.2 25.4 %all-reduce.18 = (f32[3200]{0:T(1024)S(1)}, f32[16,256]{1,0:T(8,128)}, f32[16,256]{1,0:T(8,128)}, f32[64]{0:T(128)}, f32[64]{0:T(128)}, /*index=5*/f32[64]{0:T(1...) all-reduce(f32[3200]{0:T(1024)S(1)} %dynamic-slice.14, ...), channel_id=1, replica_groups=mesh['dp'=8,'fsdp'=4] {'dp'}, use_global_device_ids=true, to_apply=%region_20.21 | all-reduce | flops 12032 | bytes 96256 | tf_op jit(solution)/shard_map/psum | solution.py:341
  830.2 60.0 %all-reduce.24.cloned.1.call-done = (f32[3200,256]{1,0:T(8,128)}, f32[512,256]{0,1:T(8,128)}, f32[64,768]{1,0:T(8,128)}, f32[64,256]{1,0:T(8,128)}, f32[64,512]{1,0:T(8,128)}, /*index=5*/f32[128,256]{1,0:T(8,128)}) async-done(((f32[3200,256]{1,0:T(8,128)}, f32[512,256]{0,1:T(8,128)}, f32[64,768]{1,0:T(8,128)}, f32[64,256]{1,0:T(8,128)}, f32[64,512]{1,0:T(8,128)}, /*index=5*/f32[128,256]{1,0:T(8,128)}), ...) | async-done | bytes 4325392 | tf_op jit(solution)/shard_map/psum | solution.py:341
  (340 shorter events, 296.4 us)
Async XLA Ops:
  7.2 160.6 %all-gather.4.cloned.1.call-start = ((), (), s32[]{:S(2)}) async-start(), calls=%async_computation.8 | async-start | bytes 8192000 | tf_op jit(solution)/shard_map/all_gather | solution.py:156
  7.9 173.8 %all-gather.6.cloned.1.call-start = ((), (), s32[]{:S(2)}) async-start(), calls=%async_computation.9 | async-start | bytes 1310720 | tf_op jit(solution)/shard_map/all_gather | solution.py:159
  9.8 503.4 %reduce-scatter.19.cloned.1.call-start = ((), (), s32[]{:S(2)}) async-start(), calls=%async_computation.15 | async-start | bytes 327680 | tf_op jit(solution)/shard_map/reduce_scatter | solution.py:313
  72.7 19.5 %copy-start.49 = (bf16[64,256]{1,0:T(8,128)(2,1)S(1)}, bf16[64,256]{1,0:T(8,128)(2,1)}, u32[]{:S(2)}) copy-start(bf16[64,256]{1,0:T(8,128)(2,1)} %param.42) | copy-start | bytes 98308
  72.7 38.4 %copy-start.44 = (bf16[64,512]{1,0:T(8,128)(2,1)S(1)}, bf16[64,512]{1,0:T(8,128)(2,1)}, u32[]{:S(2)}) copy-start(bf16[64,512]{1,0:T(8,128)(2,1)} %param.46) | copy-start | bytes 196612
  72.7 60.5 %copy-start.45 = (bf16[128,256]{1,0:T(8,128)(2,1)S(1)}, bf16[128,256]{1,0:T(8,128)(2,1)}, u32[]{:S(2)}) copy-start(bf16[128,256]{1,0:T(8,128)(2,1)} %param.48) | copy-start | bytes 196612
  73.4 94.4 %copy-start.50 = (s32[1,2048]{1,0:T(1,128)S(1)}, s32[1,2048]{1,0:T(1,128)}, u32[]{:S(2)}) copy-start(s32[1,2048]{1,0:T(1,128)} %param.27) | copy-start | bytes 24580
  150.7 31.0 %copy-start.34 = (f32[2048]{0:T(1024)}, f32[2048]{0:T(1024)S(1)}, u32[]{:S(2)}) copy-start(f32[2048]{0:T(1024)S(1)} %fusion.78) | copy-start | bytes 24580
  167.8 16.4 %copy-start.20 = (bf16[256,768]{1,0:T(8,128)(2,1)}, bf16[256,768]{1,0:T(8,128)(2,1)S(1)}, u32[]{:S(2)}) copy-start(bf16[256,768]{1,0:T(8,128)(2,1)S(1)} %all_gather.63) | copy-start | bytes 1179652
  167.8 13.9 %copy-start.63 = (f32[1,256]{1,0:T(1,128)S(1)}, f32[1,256]{1,0:T(1,128)}, u32[]{:S(2)}) copy-start(f32[1,256]{1,0:T(1,128)} %dynamic-slice_convert_fusion) | copy-start | bytes 3076
  248.9 11.5 %copy-start.4 = (f32[2048,256]{0,1:T(8,128)}, f32[2048,256]{0,1:T(8,128)S(1)}, u32[]{:S(2)}) copy-start(f32[2048,256]{0,1:T(8,128)S(1)} %get-tuple-element.435) | copy-start | bytes 6291460
  249.5 11.0 %copy-start.15 = (bf16[1,2048,256]{1,2,0:T(8,128)(2,1)S(1)}, bf16[1,2048,256]{1,2,0:T(8,128)(2,1)}, u32[]{:S(2)}) copy-start(bf16[1,2048,256]{1,2,0:T(8,128)(2,1)} %copy.83) | copy-start | bytes 3145732
  249.5 11.0 %copy-start.24 = (bf16[512,256]{1,0:T(8,128)(2,1)S(1)}, bf16[512,256]{1,0:T(8,128)(2,1)}, u32[]{:S(2)}) copy-start(bf16[512,256]{1,0:T(8,128)(2,1)} %all_gather.72) | copy-start | bytes 786436
  278.0 235.2 %reduce-scatter.21.cloned.1.call-start = ((), (), s32[]{:S(2)}) async-start(), calls=%async_computation.16 | async-start | bytes 655360 | tf_op jit(solution)/shard_map/reduce_scatter | solution.py:317
  281.9 231.4 %reduce-scatter.23.cloned.1.call-start = ((), (), s32[]{:S(2)}) async-start(), calls=%async_computation.17 | async-start | bytes 655360 | tf_op jit(solution)/shard_map/reduce_scatter | solution.py:319
  296.9 216.3 %reduce-scatter.17.cloned.1.call-start = ((), (), s32[]{:S(2)}) async-start(), calls=%async_computation.14 | async-start | bytes 983040 | tf_op jit(solution)/shard_map/reduce_scatter | solution.py:310
  472.8 66.5 %reduce-scatter.15.cloned.1.call-start = ((), (), s32[]{:S(2)}) async-start(), calls=%async_computation.13 | async-start | bytes 2621440 | tf_op jit(solution)/shard_map/reduce_scatter | solution.py:307
  487.2 274.0 %reduce-scatter.9.cloned.1.call-start = ((), (), s32[]{:S(2)}) async-start(), calls=%async_computation.10 | async-start | bytes 16384000 | tf_op jit(solution)/shard_map/reduce_scatter | solution.py:303
  508.1 292.7 %reduce-scatter.13.cloned.1.call-start = ((), (), s32[]{:S(2)}) async-start(), calls=%async_computation.12 | async-start | bytes 81920 | tf_op jit(solution)/shard_map/reduce_scatter | solution.py:306
  508.9 295.2 %reduce-scatter.11.cloned.1.call-start = ((), (), s32[]{:S(2)}) async-start(), calls=%async_computation.11 | async-start | bytes 81920 | tf_op jit(solution)/shard_map/reduce_scatter | solution.py:305
  509.2 265.3 %copy-start.71 = (bf16[256]{0:T(256)(128)(2,1)S(1)}, bf16[256]{0:T(256)(128)(2,1)}, u32[]{:S(2)}) copy-start(bf16[256]{0:T(256)(128)(2,1)} %get-tuple-element.412) | copy-start | bytes 1540
  509.2 265.3 %copy-start.6 = (f32[2048,256]{0,1:T(8,128)S(1)}, f32[2048,256]{0,1:T(8,128)}, u32[]{:S(2)}) copy-start(f32[2048,256]{0,1:T(8,128)} %copy-done.4) | copy-start | bytes 6291460
  509.2 265.3 %copy-start.25 = (bf16[512,256]{1,0:T(8,128)(2,1)S(1)}, bf16[512,256]{1,0:T(8,128)(2,1)}, u32[]{:S(2)}) copy-start(bf16[512,256]{1,0:T(8,128)(2,1)} %all_gather.72) | copy-start | bytes 786436
  513.1 377.1 %all-reduce.24.cloned.1.call-start = ((), (), s32[]{:S(2)}) async-start(), calls=%async_computation.18 | async-start | bytes 8650752 | tf_op jit(solution)/shard_map/psum | solution.py:341
  (63 other events, 219.0 us)
Sparse Core Ops, SparseCore 0:
  9.6 133.5 all-gather.3
  145.3 29.6 all-gather.5
  278.1 16.6 reduce-scatter.18
  297.6 19.8 reduce-scatter.20
  319.8 19.8 reduce-scatter.22
  472.9 20.1 reduce-scatter.16
  496.1 43.1 reduce-scatter.14
  541.6 219.6 reduce-scatter.8
  764.1 20.0 reduce-scatter.12
  786.9 17.1 reduce-scatter.10
  808.0 82.1 all-reduce.23
where the time goes:
time: 911 us; the launch traced here: 906 us
  waiting for transfers between devices  312 us (34%)
  matrix products  201 us (22%)
  blocking collectives  176 us (19%)
  other arithmetic  119 us (13%)
  local copies, waits for them, and re-layouts  77.5 us (9%)
  between operations  19.1 us (2%)
    reduce_scatter x1, waiting for transfers between devices, body(): lax.psum_scatter(dense_grad, 'fsdp', scatter_dimension=0, tiled=True)  222 us
    psum x1, waiting for transfers between devices, body(): lax.psum((table_share, count_share, expr_share, study_share, position_sha...  60 us
    convert_element_type x4, other arithmetic, one_block(): grad_scores = (probs * (grad_probs - inner)).astype(jnp.bfloat16)  42.7 us
    dot_general x4, matrix products, one_block(): jnp.einsum('qhk,shk->hqs', grad_block, values, preferred_element_type=jnp...  38.1 us
    unnamed x185, local copies, waits for them, and re-layouts  37.2 us
    unnamed x2, blocking collectives  35.6 us
    dot_general x4, matrix products, one_block(): jnp.einsum('hqs,shk->qhk', grad_scores, keys, preferred_element_type=jnp....  27.6 us
    dot_general x8, matrix products, one_block(): jnp.einsum('qhk,shk->hqs', query_block, keys, preferred_element_type=jnp....  27.3 us
  transfers between devices with their start and end apart: 11, of which 4 were waited for; matrix products, arithmetic and copies ran while one was open for 32% of the time, Pallas kernels for 0%

commit v1 on v0

--- a/solution.py
+++ b/solution.py
@@ -6,6 +6,12 @@
 HEADS = 4
 epsilon = 1e-05
 highest = lax.Precision.HIGHEST
+
+
+def gather_from_all(x, axis, dim):
+    size = lax.axis_size(axis)
+    repeats = [size if d == dim else 1 for d in range(x.ndim)]
+    return lax.all_to_all(jnp.tile(x, repeats), axis, split_axis=dim, concat_axis=dim, tiled=True)
 
 
 def normalize(values):
@@ -162,7 +168,7 @@
         lax.all_gather(w_qkv, "fsdp", axis=0, tiled=True),
         lax.all_gather(bias_query, "fsdp", axis=0, tiled=True),
         lax.all_gather(bias_value, "fsdp", axis=0, tiled=True),
-        lax.all_gather(w_output, "fsdp", axis=0, tiled=True),
+        gather_from_all(w_output, "fsdp", 0),
         lax.all_gather(bias_output, "fsdp", axis=0, tiled=True),
         lax.all_gather(norm2_gain, "fsdp", axis=0, tiled=True),
         lax.all_gather(norm2_shift, "fsdp", axis=0, tiled=True),

time: 911 us -> 920 us (level)
    unnamed x185 -> x179, local copies, waits for them, and re-layouts: 37.2 us -> 38.8 us
  transfers between devices with their start and end apart: 11 -> 12, of which waited for: 4 -> 5; matrix products, arithmetic and copies ran while one was open for 32% -> 39% of each run, Pallas kernels for 0% -> 0%
where the time goes in v1:
time: 920 us; the launch traced here: 915 us
  waiting for transfers between devices  320 us (35%)
  matrix products  202 us (22%)
  blocking collectives  167 us (18%)
  other arithmetic  119 us (13%)
  local copies, waits for them, and re-layouts  80.5 us (9%)
  between operations  19 us (2%)
    reduce_scatter x1, waiting for transfers between devices, body(): lax.psum_scatter(dense_grad, 'fsdp', scatter_dimension=0, tiled=True)  222 us
    psum x1, waiting for transfers between devices, body(): lax.psum((table_share, count_share, expr_share, study_share, position_sha...  60.2 us
    convert_element_type x4, other arithmetic, one_block(): grad_scores = (probs * (grad_probs - inner)).astype(jnp.bfloat16)  42.6 us
    unnamed x179, local copies, waits for them, and re-layouts  38.8 us
    dot_general x4, matrix products, one_block(): jnp.einsum('qhk,shk->hqs', grad_block, values, preferred_element_type=jnp...  37.6 us
    unnamed x2, blocking collectives  32.4 us
    reduce_scatter x1, waiting for transfers between devices, body(): lax.psum_scatter(grad_position, 'fsdp', scatter_dimension=0, tiled=True)  28.3 us
    dot_general x4, matrix products, one_block(): jnp.einsum('hqs,shk->qhk', grad_scores, keys, preferred_element_type=jnp....  27.6 us
  transfers between devices with their start and end apart: 12, of which 5 were waited for; matrix products, arithmetic and copies ran while one was open for 39% of the time, Pallas kernels for 0%

profile of v1, /device:TPU:0, one launch (start us, length us, event | category | flops | bytes accessed | tf_op | source)
XLA Modules:
  0.0 914.7 jit_solution(17489912226179058836)
XLA Ops:
  28.4 13.0 %all-reduce.21 = (bf16[256]{0:T(256)(128)(2,1)S(1)}, bf16[256]{0:T(256)(128)(2,1)S(1)}, bf16[256]{0:T(256)(128)(2,1)S(1)}, bf16[256]{0:T(256)(128)(2,1)S(1)}, bf...) all-reduce(bf16[256]{0:T(256)(128)(2,1)S(1)} %dynamic-update-slice., ...), channel_id=1, replica_groups=mesh['dp'=8,'fsdp'=4] {'fsdp'}, use_global_device_ids=true, to_apply=%add.1 | all-reduce | flops 2048 | bytes 8192
  45.2 11.1 %all-gather = bf16[4,1,128]{2,1,0:T(2,128)(2,1)S(1)} all-gather(bf16[1,1,128]{2,1,0:T(2,128)(2,1)} %bitcast.193), channel_id=1, replica_groups=mesh['dp'=8,'fsdp'=4] {'fsdp'}, dimensions={0}, use_global_device_ids=true | all-gather | bytes 1280 | tf_op jit(solution)/shard_map/all_gather | solution.py:176
  56.9 15.9 %all_gather.57 = bf16[64,256]{1,0:T(8,128)(2,1)S(1)} all-gather(bf16[16,256]{1,0:T(8,128)(2,1)} %param.34), channel_id=1, replica_groups=mesh['dp'=8,'fsdp'=4] {'fsdp'}, dimensions={0}, use_global_device_ids=true | all-gather | bytes 40960 | tf_op jit(solution)/shard_map/all_gather | solution.py:163
  83.9 15.9 %all_gather.58 = bf16[64,256]{1,0:T(8,128)(2,1)S(1)} all-gather(bf16[16,256]{1,0:T(8,128)(2,1)S(1)} %copy-done.52), channel_id=1, replica_groups=mesh['dp'=8,'fsdp'=4] {'fsdp'}, dimensions={0}, use_global_device_ids=true | all-gather | bytes 40960 | tf_op jit(solution)/shard_map/all_gather | solution.py:164
  99.8 20.6 %all_gather.68 = bf16[256,512]{1,0:T(8,128)(2,1)} all-gather(bf16[64,512]{1,0:T(8,128)(2,1)S(1)} %copy-done.42), channel_id=1, replica_groups=mesh['dp'=8,'fsdp'=4] {'fsdp'}, dimensions={0}, use_global_device_ids=true | all-gather | bytes 327680 | tf_op jit(solution)/shard_map/all_gather | solution.py:175
  120.4 16.7 %all_gather.70 = bf16[512,256]{1,0:T(8,128)(2,1)} all-gather(bf16[128,256]{1,0:T(8,128)(2,1)S(1)} %copy-done.43), channel_id=1, replica_groups=mesh['dp'=8,'fsdp'=4] {'fsdp'}, dimensions={0}, use_global_device_ids=true | all-gather | bytes 327680 | tf_op jit(solution)/shard_map/all_gather | solution.py:177
  137.7 15.0 %all_gather.62 = bf16[256,768]{1,0:T(8,128)(2,1)S(1)} all-gather(bf16[64,768]{1,0:T(8,128)(2,1)} %param.39), channel_id=1, replica_groups=mesh['dp'=8,'fsdp'=4] {'fsdp'}, dimensions={0}, use_global_device_ids=true | all-gather | bytes 491520 | tf_op jit(solution)/shard_map/all_gather | solution.py:168
  152.8 12.3 %gather_fusion = bf16[2048,256]{1,0:T(8,128)(2,1)} fusion(bf16[12800,256]{1,0:T(8,128)(2,1)} %all-gather.4.cloned.1.call-done, s32[2048]{0:T(1024)S(1)} %broadcast_clamp_fusion.1), kind=kCustom, calls=%fused_computation | custom fusion | bytes 2105344 | tf_op jit(solution)/shard_map/gather | solution.py:195
  183.0 53.9 %while.49 = (s32[]{:T(128)}, bf16[4,512,4,64]{1,3,2,0:T(8,128)(2,1)}, f32[4,4,512]{2,1,0:T(4,128)S(1)}, bf16[4,512,4,64]{1,3,2,0:T(8,128)(2,1)}, bf16[2048,4,64]...) while((s32[]{:T(128)}, bf16[4,512,4,64]{1,3,2,0:T(8,128)(2,1)}, ...), condition=%wide.region_5.6_spmd.clone, body=%wide.region_2.5_spmd.clone.sunk | while | flops 1124208640 | bytes 53026924 | solution.py:70
  243.1 10.9 %multiply_convert_fusion.1 = (bf16[2048,512]{1,0:T(8,128)(2,1)}, f32[2048,512]{1,0:T(8,128)S(1)}, f32[2048,512]{1,0:T(8,128)S(1)}) fusion(f32[512]{0:T(512)S(1)} %bitcast.191, bf16[256,512]{1,0:T(8,128)(2,1)S(1)} %copy-done.23, f32[2048,256]{0,1:T(8,128)S(1)} %get-tuple-element.435, f32[256]{0:T(256)S(1)} %copy-done.69, f32[256]{0:T(256)S(1)} %copy-done.61, ...), kind=kOutput, calls=%fused_computation.63 | convolution fusion | flops 608698368 | bytes 12865536 | tf_op jit(solution)/shard_map/dot_general | solution.py:31
  275.5 14.0 %all_gather.72 = bf16[256,256]{1,0:T(8,128)(2,1)S(1)} all-gather(bf16[64,256]{1,0:T(8,128)(2,1)S(1)} %copy-done.35), channel_id=1, replica_groups=mesh['dp'=8,'fsdp'=4] {'fsdp'}, dimensions={0}, use_global_device_ids=true | all-gather | bytes 163840 | tf_op jit(solution)/shard_map/all_gather | solution.py:228
  304.4 166.1 %while.50 = (s32[]{:T(128)}, f32[2048,4,64]{0,2,1:T(8,128)}, f32[2048,4,64]{0,2,1:T(8,128)}, bf16[4,512,4,64]{1,3,2,0:T(8,128)(2,1)}, bf16[4,512,4,64]{1,3,2,0:T...) while((s32[]{:T(128)}, f32[2048,4,64]{0,2,1:T(8,128)}, ...), condition=%wide.region_12.13_spmd.clone, body=%wide.region_10.12_spmd.clone.sunk | while | flops 2750025728 | bytes 172556464 | solution.py:112
  314.2 9.4 %multiply_reduce_fusion.8 = (f32[4,512]{1,0:T(4,128)S(1)}, f32[4,512,2048]{2,1,0:T(8,128)}) fusion(f32[4,512,2048]{2,1,0:T(8,128)S(1)} %fusion.154, f32[4,512]{1,0:T(4,128)S(1)} %dynamic-slice_bitcast_fusion.2, pred[2048]{0:T(1024)(128)(4,1)S(1)} %convert_compare_fusion.5, bf16[2048,4,64]{0,2,1:T(8,128)(2,1)S(1)} %get-tuple-element.611, ...), kind=kOutput, calls=%fused_computation.25.clone.1 | convolution fusion | flops 557840384 | bytes 34883588 | tf_op jit(solution)/shard_map/while/body/eval_jaxpr/while/body/eval_jaxpr/qhk,shk->hqs/dot_general | solution.py:90
  323.6 10.7 %multiply_convert_fusion.3 = bf16[4,512,2048]{2,1,0:T(8,128)(2,1)} fusion(f32[4,512,2048]{2,1,0:T(8,128)} %get-tuple-element.553, f32[4,512,2048]{2,1,0:T(8,128)S(1)} %fusion.154, f32[4,512]{1,0:T(4,128)S(1)} %get-tuple-element.554, f32[4,512]{1,0:T(4,128)S(1)} %dynamic-slice_bitcast_fusion.2, pred[2048]{0:T(1024)(128)(4,1)S(1)} %convert_compare_fusion.5), kind=kLoop, calls=%fused_computation.24.clone.1 | loop fusion | flops 25165824 | bytes 41961472 | tf_op jit(solution)/shard_map/while/body/eval_jaxpr/while/body/eval_jaxpr/convert_element_type | solution.py:94
  364.7 10.6 %multiply_convert_fusion.3 = bf16[4,512,2048]{2,1,0:T(8,128)(2,1)} fusion(f32[4,512,2048]{2,1,0:T(8,128)} %get-tuple-element.553, f32[4,512,2048]{2,1,0:T(8,128)S(1)} %fusion.154, f32[4,512]{1,0:T(4,128)S(1)} %get-tuple-element.554, f32[4,512]{1,0:T(4,128)S(1)} %dynamic-slice_bitcast_fusion.2, pred[2048]{0:T(1024)(128)(4,1)S(1)} %convert_compare_fusion.5), kind=kLoop, calls=%fused_computation.24.clone.1 | loop fusion | flops 25165824 | bytes 41961472 | tf_op jit(solution)/shard_map/while/body/eval_jaxpr/while/body/eval_jaxpr/convert_element_type | solution.py:94
  406.5 10.6 %multiply_convert_fusion.3 = bf16[4,512,2048]{2,1,0:T(8,128)(2,1)} fusion(f32[4,512,2048]{2,1,0:T(8,128)} %get-tuple-element.553, f32[4,512,2048]{2,1,0:T(8,128)S(1)} %fusion.154, f32[4,512]{1,0:T(4,128)S(1)} %get-tuple-element.554, f32[4,512]{1,0:T(4,128)S(1)} %dynamic-slice_bitcast_fusion.2, pred[2048]{0:T(1024)(128)(4,1)S(1)} %convert_compare_fusion.5), kind=kLoop, calls=%fused_computation.24.clone.1 | loop fusion | flops 25165824 | bytes 41961472 | tf_op jit(solution)/shard_map/while/body/eval_jaxpr/while/body/eval_jaxpr/convert_element_type | solution.py:94
  448.2 10.6 %multiply_convert_fusion.3 = bf16[4,512,2048]{2,1,0:T(8,128)(2,1)} fusion(f32[4,512,2048]{2,1,0:T(8,128)} %get-tuple-element.553, f32[4,512,2048]{2,1,0:T(8,128)S(1)} %fusion.154, f32[4,512]{1,0:T(4,128)S(1)} %get-tuple-element.554, f32[4,512]{1,0:T(4,128)S(1)} %dynamic-slice_bitcast_fusion.2, pred[2048]{0:T(1024)(128)(4,1)S(1)} %convert_compare_fusion.5), kind=kLoop, calls=%fused_computation.24.clone.1 | loop fusion | flops 25165824 | bytes 41961472 | tf_op jit(solution)/shard_map/while/body/eval_jaxpr/while/body/eval_jaxpr/convert_element_type | solution.py:94
  497.3 17.5 %scatter_custom_fusion = f32[12800,256]{1,0:T(8,128)} fusion(s32[2048]{0:T(1024)S(1)} %bitcast.188, f32[2048,256]{1,0:T(8,128)} %copy.90, f32[]{:T(128)} %constant.51.clone.1), kind=kCustom, calls=%fused_computation.57 | custom fusion | flops 524288 | bytes 13107712 | tf_op jit(solution)/shard_map/scatter-add | solution.py:287
  520.0 28.3 %reduce-scatter.15.cloned.1.call-done = f32[512,256]{0,1:T(8,128)} async-done(((f32[2048,256]{0,1:T(8,128)}), f32[512,256]{0,1:T(8,128)}) %reduce-scatter.15.cloned.1.call-update) | async-done | bytes 524304 | tf_op jit(solution)/shard_map/reduce_scatter | solution.py:313
  548.3 222.0 %reduce-scatter.9.cloned.1.call-done = f32[3200,256]{1,0:T(8,128)} async-done(((f32[12800,256]{1,0:T(8,128)}), f32[3200,256]{1,0:T(8,128)}) %reduce-scatter.9.cloned.1.call-update) | async-done | bytes 3276816 | tf_op jit(solution)/shard_map/reduce_scatter | solution.py:309
  770.3 11.3 %scatter_custom_fusion.1 = f32[12800]{0:T(1024)S(1)} fusion(s32[2048]{0:T(1024)S(1)} %bitcast.189, f32[2048]{0:T(1024)S(1)} %copy-done.33, f32[]{:T(128)} %constant.51.clone.1), kind=kCustom, calls=%fused_computation.126 | custom fusion | flops 2048 | bytes 51204 | tf_op jit(solution)/shard_map/scatter-add | solution.py:288
  789.7 19.5 %all-reduce.20 = (f32[12800]{0:T(1024)S(1)}, f32[256]{0:T(256)S(1)}, f32[256]{0:T(256)S(1)}, f32[256]{0:T(256)S(1)}, f32[256]{0:T(256)S(1)}, /*index=5*/f32[256]...) all-reduce(f32[12800]{0:T(1024)S(1)} %scatter_custom_fusion.1, ...), channel_id=3, replica_groups=mesh['dp'=8,'fsdp'=4] {'fsdp'}, use_global_device_ids=true, to_apply=%region_19.20.clone | all-reduce | flops 15360 | bytes 122880
  813.2 25.4 %all-reduce.18 = (f32[3200]{0:T(1024)S(1)}, f32[16,256]{1,0:T(8,128)}, f32[16,256]{1,0:T(8,128)}, f32[64]{0:T(128)}, f32[64]{0:T(128)}, /*index=5*/f32[64]{0:T(1...) all-reduce(f32[3200]{0:T(1024)S(1)} %dynamic-slice.14, ...), channel_id=1, replica_groups=mesh['dp'=8,'fsdp'=4] {'dp'}, use_global_device_ids=true, to_apply=%region_20.21 | all-reduce | flops 12032 | bytes 96256 | tf_op jit(solution)/shard_map/psum | solution.py:347
  839.2 60.2 %all-reduce.24.cloned.1.call-done = (f32[3200,256]{1,0:T(8,128)}, f32[512,256]{0,1:T(8,128)}, f32[64,768]{1,0:T(8,128)}, f32[64,256]{1,0:T(8,128)}, f32[64,512]{1,0:T(8,128)}, /*index=5*/f32[128,256]{1,0:T(8,128)}) async-done(((f32[3200,256]{1,0:T(8,128)}, f32[512,256]{0,1:T(8,128)}, f32[64,768]{1,0:T(8,128)}, f32[64,256]{1,0:T(8,128)}, f32[64,512]{1,0:T(8,128)}, /*index=5*/f32[128,256]{1,0:T(8,128)}), ...) | async-done | bytes 4325392 | tf_op jit(solution)/shard_map/psum | solution.py:347
  (337 shorter events, 313.9 us)
Async XLA Ops:
  7.2 145.6 %all-gather.4.cloned.1.call-start = ((), (), s32[]{:S(2)}) async-start(), calls=%async_computation.9 | async-start | bytes 8192000 | tf_op jit(solution)/shard_map/all_gather | solution.py:162
  9.3 230.8 %all-to-all-start = ((bf16[4,64,256]{2,1,0:T(8,128)(2,1)}), bf16[4,64,256]{2,1,0:T(8,128)(2,1)}, u32[]{:S(2)}, u32[]{:S(2)}) async-start(bf16[4,64,256]{2,1,0:T(8,128)(2,1)} %tile.2), calls=%async_computation | async-start | bytes 262144 | tf_op jit(solution)/shard_map/all_to_all | solution.py:14
  15.7 156.2 %all-gather.6.cloned.1.call-start = ((), (), s32[]{:S(2)}) async-start(), calls=%async_computation.10 | async-start | bytes 1310720 | tf_op jit(solution)/shard_map/all_gather | solution.py:165
  17.5 502.4 %reduce-scatter.19.cloned.1.call-start = ((), (), s32[]{:S(2)}) async-start(), calls=%async_computation.16 | async-start | bytes 327680 | tf_op jit(solution)/shard_map/reduce_scatter | solution.py:319
  80.3 19.6 %copy-start.42 = (bf16[64,512]{1,0:T(8,128)(2,1)S(1)}, bf16[64,512]{1,0:T(8,128)(2,1)}, u32[]{:S(2)}) copy-start(bf16[64,512]{1,0:T(8,128)(2,1)} %param.46) | copy-start | bytes 196612
  80.3 40.1 %copy-start.43 = (bf16[128,256]{1,0:T(8,128)(2,1)S(1)}, bf16[128,256]{1,0:T(8,128)(2,1)}, u32[]{:S(2)}) copy-start(bf16[128,256]{1,0:T(8,128)(2,1)} %param.48) | copy-start | bytes 196612
  81.0 71.7 %copy-start.47 = (s32[1,2048]{1,0:T(1,128)S(1)}, s32[1,2048]{1,0:T(1,128)}, u32[]{:S(2)}) copy-start(s32[1,2048]{1,0:T(1,128)} %param.27) | copy-start | bytes 24580
  137.7 34.1 %copy-start.31 = (f32[2048]{0:T(1024)}, f32[2048]{0:T(1024)S(1)}, u32[]{:S(2)}) copy-start(f32[2048]{0:T(1024)S(1)} %fusion.78) | copy-start | bytes 24580
  152.7 21.6 %copy-start.18 = (bf16[256,768]{1,0:T(8,128)(2,1)}, bf16[256,768]{1,0:T(8,128)(2,1)S(1)}, u32[]{:S(2)}) copy-start(bf16[256,768]{1,0:T(8,128)(2,1)S(1)} %all_gather.62) | copy-start | bytes 1179652
  152.7 19.1 %copy-start.60 = (f32[1,256]{1,0:T(1,128)S(1)}, f32[1,256]{1,0:T(1,128)}, u32[]{:S(2)}) copy-start(f32[1,256]{1,0:T(1,128)} %dynamic-slice_convert_fusion) | copy-start | bytes 3076
  242.7 11.3 %copy-start.3 = (f32[2048,256]{0,1:T(8,128)}, f32[2048,256]{0,1:T(8,128)S(1)}, u32[]{:S(2)}) copy-start(f32[2048,256]{0,1:T(8,128)S(1)} %get-tuple-element.435) | copy-start | bytes 6291460
  243.0 10.9 %copy-start.13 = (bf16[1,2048,256]{1,2,0:T(8,128)(2,1)S(1)}, bf16[1,2048,256]{1,2,0:T(8,128)(2,1)}, u32[]{:S(2)}) copy-start(bf16[1,2048,256]{1,2,0:T(8,128)(2,1)} %copy.83) | copy-start | bytes 3145732
  243.1 10.9 %copy-start.21 = (bf16[512,256]{1,0:T(8,128)(2,1)S(1)}, bf16[512,256]{1,0:T(8,128)(2,1)}, u32[]{:S(2)}) copy-start(bf16[512,256]{1,0:T(8,128)(2,1)} %all_gather.70) | copy-start | bytes 786436
  271.5 248.4 %reduce-scatter.21.cloned.1.call-start = ((), (), s32[]{:S(2)}) async-start(), calls=%async_computation.17 | async-start | bytes 655360 | tf_op jit(solution)/shard_map/reduce_scatter | solution.py:323
  275.4 244.6 %reduce-scatter.23.cloned.1.call-start = ((), (), s32[]{:S(2)}) async-start(), calls=%async_computation.18 | async-start | bytes 655360 | tf_op jit(solution)/shard_map/reduce_scatter | solution.py:325
  304.4 215.6 %reduce-scatter.17.cloned.1.call-start = ((), (), s32[]{:S(2)}) async-start(), calls=%async_computation.15 | async-start | bytes 983040 | tf_op jit(solution)/shard_map/reduce_scatter | solution.py:316
  479.5 68.8 %reduce-scatter.15.cloned.1.call-start = ((), (), s32[]{:S(2)}) async-start(), calls=%async_computation.14 | async-start | bytes 2621440 | tf_op jit(solution)/shard_map/reduce_scatter | solution.py:313
  493.9 276.4 %reduce-scatter.9.cloned.1.call-start = ((), (), s32[]{:S(2)}) async-start(), calls=%async_computation.11 | async-start | bytes 16384000 | tf_op jit(solution)/shard_map/reduce_scatter | solution.py:309
  514.8 295.0 %reduce-scatter.13.cloned.1.call-start = ((), (), s32[]{:S(2)}) async-start(), calls=%async_computation.13 | async-start | bytes 81920 | tf_op jit(solution)/shard_map/reduce_scatter | solution.py:312
  515.6 297.5 %reduce-scatter.11.cloned.1.call-start = ((), (), s32[]{:S(2)}) async-start(), calls=%async_computation.12 | async-start | bytes 81920 | tf_op jit(solution)/shard_map/reduce_scatter | solution.py:311
  515.9 267.6 %copy-start.68 = (bf16[256]{0:T(256)(128)(2,1)S(1)}, bf16[256]{0:T(256)(128)(2,1)}, u32[]{:S(2)}) copy-start(bf16[256]{0:T(256)(128)(2,1)} %get-tuple-element.412) | copy-start | bytes 1540
  515.9 267.6 %copy-start.5 = (f32[2048,256]{0,1:T(8,128)S(1)}, f32[2048,256]{0,1:T(8,128)}, u32[]{:S(2)}) copy-start(f32[2048,256]{0,1:T(8,128)} %copy-done.3) | copy-start | bytes 6291460
  515.9 267.6 %copy-start.22 = (bf16[512,256]{1,0:T(8,128)(2,1)S(1)}, bf16[512,256]{1,0:T(8,128)(2,1)}, u32[]{:S(2)}) copy-start(bf16[512,256]{1,0:T(8,128)(2,1)} %all_gather.70) | copy-start | bytes 786436
  519.8 379.5 %all-reduce.24.cloned.1.call-start = ((), (), s32[]{:S(2)}) async-start(), calls=%async_computation.19 | async-start | bytes 8650752 | tf_op jit(solution)/shard_map/psum | solution.py:347
  (61 other events, 227.9 us)
Sparse Core Ops, SparseCore 0:
  9.6 133.9 all-gather.3
  145.7 26.0 all-gather.5
  271.6 19.7 reduce-scatter.18
  294.2 19.8 reduce-scatter.20
  316.4 19.8 reduce-scatter.22
  479.6 22.4 reduce-scatter.16
  505.1 43.1 reduce-scatter.14
  550.7 219.5 reduce-scatter.8
  773.1 20.0 reduce-scatter.12
  795.9 17.1 reduce-scatter.10
  817.0 82.2 all-reduce.23
